TPU v7x, 32 devices: a whole 2x2x4 slice. The times are simulated.
32 devices in a mesh: shot: 2 (over y), gx: 4 (over z), gy: 4 (over x, core).
Axes of the slice: x: 2, y: 2, z: 4, core: 2. Of those that a mesh axis runs over, the one named last changes fastest.
Arguments:
- source_prev: float32 [64, 32, 320], P(('shot', 'gx'), 'gy'), parts along dimension 0, may hold values from -0.6 to 0.6
- source_now: float32 [64, 32, 320], P(('shot', 'gx'), 'gy'), parts along dimension 0, may hold values from -0.6 to 0.6
- receiver_prev: float32 [64, 32, 320], P(('shot', 'gx'), 'gy'), parts along dimension 0, may hold values from -6 to 6
- receiver_now: float32 [64, 32, 320], P(('shot', 'gx'), 'gy'), parts along dimension 0, may hold values from -6 to 6
- speed_squared: float32 [64, 32, 320], P(('shot', 'gx'), 'gy'), parts along dimension 0, may hold values from 0.05 to 0.18
- wavelet: float32 [20], P('shot'), parts along dimension 0, may hold values from -40 to 40
- source_cell: int32 [2], P('shot'), parts along dimension 0, may hold values from 0 to 327679
- traces: float32 [20, 1024], P('shot', ('gx', 'gy')), parts along dimension 0, may hold values from -18 to 18
- receiver_cells: int32 [2, 1024], P('shot', ('gx', 'gy')), parts along dimension 0, may hold values from 0 to 1023
- plan: int32 [8], P('shot'), parts along dimension 0, may hold values from 0 to 9, as said below
- stored_snapshots: bfloat16 [8, 32, 32, 320], P('shot', 'gx', 'gy'), parts along dimension 0, may hold values from -6 to 6
- image_before: float32 [64, 32, 320], P(('shot', 'gx'), 'gy'), parts along dimension 0, may hold values from -6 to 6
Outputs:
- new_source_prev: float32 [64, 32, 320], P(('shot', 'gx'), 'gy'), parts along dimension 0
- new_source_now: float32 [64, 32, 320], P(('shot', 'gx'), 'gy'), parts along dimension 0
- new_receiver_prev: float32 [64, 32, 320], P(('shot', 'gx'), 'gy'), parts along dimension 0
- new_receiver_now: float32 [64, 32, 320], P(('shot', 'gx'), 'gy'), parts along dimension 0
- snapshots: bfloat16 [8, 32, 32, 320], P('shot', 'gx', 'gy'), parts along dimension 0
- image: float32 [64, 32, 320], P(('shot', 'gx'), 'gy'), parts along dimension 0
There are 2 independent parts, one for each index of `shot`. A program takes and returns all parts, laid end to end along the dimension named above; each array names one. Nothing has to cross between parts.
Inputs may be any that keep to these rules, and one draw needn't show every extreme that they name: `plan`: 4 different steps in increasing order; the first is 0 and the last is 9.
All inputs are finite; a program needn't handle non-finite values.
Results may differ from a plain program's by a relative error of at most 0.001.
Values sent between devices are 32-bit elements; how exact they have to be, the bound alone decides.
A program may use at most 64 MiB of HBM per device.

v0:
```python
import jax
import jax.numpy as jnp
from jax import lax
from jax.sharding import PartitionSpec as P

STENCIL_COEFFS = (-205.0 / 72.0, 8.0 / 5.0, -1.0 / 5.0, 8.0 / 315.0, -1.0 / 560.0)


def with_halo(block, sides, width):
    for axis, dim in sides:
        count = lax.axis_size(axis)
        forward = [(i, i + 1) for i in range(count - 1)]
        backward = [(target, source) for source, target in forward]
        low = lax.ppermute(
            lax.slice_in_dim(block, block.shape[dim] - width, None, axis=dim), axis, forward
        )
        high = lax.ppermute(lax.slice_in_dim(block, 0, width, axis=dim), axis, backward)
        block = jnp.concatenate([low, block, high], axis=dim)
    return block


def stencil(padded):
    span_x = padded.shape[0] - 8
    span_y = padded.shape[1] - 8
    depth_cells = padded.shape[2]
    deepened = jnp.pad(padded, ((0, 0), (0, 0), (4, 4)))

    def window(shift_x, shift_y, shift_z):
        return deepened[
            4 + shift_x : 4 + shift_x + span_x,
            4 + shift_y : 4 + shift_y + span_y,
            4 + shift_z : 4 + shift_z + depth_cells,
        ]

    summed = 3.0 * STENCIL_COEFFS[0] * window(0, 0, 0)
    for distance in range(1, 5):
        neighbours = window(distance, 0, 0) + window(-distance, 0, 0)
        neighbours = neighbours + window(0, distance, 0) + window(0, -distance, 0)
        neighbours = neighbours + window(0, 0, distance) + window(0, 0, -distance)
        summed = summed + STENCIL_COEFFS[distance] * neighbours
    return summed


def body(
    source_prev,
    source_now,
    receiver_prev,
    receiver_now,
    speed_squared,
    wavelet,
    source_cell,
    traces,
    receiver_cells,
    plan,
    stored_snapshots,
    image_before,
):
    block_x, block_y, depth_cells = source_now.shape
    grid_y = block_y * lax.axis_size("gy")
    start_x = lax.axis_index("gx") * block_x
    start_y = lax.axis_index("gy") * block_y
    total_steps = wavelet.shape[0]
    slot_count = plan.shape[0]
    border = 0
    span_x = block_x + 2 * border
    span_y = block_y + 2 * border
    plane_cells = span_x * span_y
    values = lax.all_gather(traces, ("gx", "gy"), axis=1, tiled=True)
    cell_ids = lax.all_gather(receiver_cells, ("gx", "gy"), axis=1, tiled=True)
    cell_ids = cell_ids[0]
    local_x = cell_ids // grid_y - (start_x - border)
    local_y = cell_ids % grid_y - (start_y - border)
    in_block = (local_x >= 0) & (local_x < span_x) & (local_y >= 0) & (local_y < span_y)
    local_cell = jnp.where(in_block, local_x * span_y + local_y, plane_cells)
    injected = (
        jnp.zeros((total_steps, plane_cells), jnp.float32)
        .at[:, local_cell]
        .add(values, mode="drop")
    )
    injected = injected.reshape(total_steps, span_x, span_y)
    snapshots = jnp.zeros(stored_snapshots.shape, jnp.bfloat16)
    imaged = image_before
    along_x = start_x - 0 + lax.broadcasted_iota(jnp.int32, (block_x + 2 * 0, 1, 1), 0)
    along_y = start_y - 0 + lax.broadcasted_iota(jnp.int32, (1, block_y + 2 * 0, 1), 1)
    along_x, along_y = (along_x, along_y)
    along_z = lax.broadcasted_iota(jnp.int32, (1, 1, depth_cells), 2)
    cell_id = source_cell[0]
    matches = (along_x == cell_id // (grid_y * depth_cells)) & (
        along_y == cell_id // depth_cells % grid_y
    )
    matches = matches & (along_z == cell_id % depth_cells)
    source_core = matches.astype(jnp.float32)
    source_before, source_field = (source_prev, source_now)
    receiver_before, receiver_field = (receiver_prev, receiver_now)
    for step_index in range(total_steps):
        back_time = total_steps - 1 - step_index
        padded = with_halo(jnp.stack([source_field, receiver_field]), (("gx", 1), ("gy", 2)), 4)
        source_spread = stencil(padded[0]) + wavelet[step_index] * source_core
        receiver_spread = stencil(padded[1]).at[:, :, 0].add(injected[back_time])
        source_latest = 2.0 * source_field - source_before + speed_squared * source_spread
        receiver_latest = 2.0 * receiver_field - receiver_before + speed_squared * receiver_spread
        source_before, source_field = (source_field, source_latest)
        receiver_before, receiver_field = (receiver_field, receiver_latest)
        record_matches = plan == step_index
        snapshots = jnp.where(
            record_matches[:, None, None, None], source_field.astype(jnp.bfloat16)[None], snapshots
        )
        correlate_matches = plan == back_time
        slot_index = jnp.sum(
            jnp.where(correlate_matches, jnp.arange(slot_count, dtype=jnp.int32), 0)
        )
        present = jnp.any(correlate_matches)
        snapshot = lax.dynamic_index_in_dim(stored_snapshots, slot_index, 0, keepdims=False).astype(
            jnp.float32
        )
        imaged = imaged + jnp.where(present, snapshot * receiver_field, 0.0)
    source_last, source_final = (source_before, source_field)
    previous, current = (receiver_before, receiver_field)
    return (source_last, source_final, previous, current, snapshots, imaged)


def solution(mesh):
    placed = (
        P(("shot", "gx"), "gy", None),
        P(("shot", "gx"), "gy", None),
        P(("shot", "gx"), "gy", None),
        P(("shot", "gx"), "gy", None),
        P(("shot", "gx"), "gy", None),
        P("shot"),
        P("shot"),
        P("shot", ("gx", "gy")),
        P("shot", ("gx", "gy")),
        P("shot"),
        P("shot", "gx", "gy", None),
        P(("shot", "gx"), "gy", None),
    )
    return jax.shard_map(
        body,
        mesh=mesh,
        in_specs=placed,
        out_specs=(
            P(("shot", "gx"), "gy", None),
            P(("shot", "gx"), "gy", None),
            P(("shot", "gx"), "gy", None),
            P(("shot", "gx"), "gy", None),
            P("shot", "gx", "gy", None),
            P(("shot", "gx"), "gy", None),
        ),
        check_vma=False,
    )
```

profile of v0, /device:TPU:18, one launch (start us, length us, event | category | flops | bytes accessed | tf_op | source)
XLA Modules:
  0.0 254.4 jit_solution(9579591347282151355)
XLA Ops:
  4.1 3.5 %collective-permute-start = (f32[2,4,8,320]{3,2,1,0:T(8,128)S(1)}, f32[2,4,8,320]{3,2,1,0:T(8,128)S(1)}, u32[]{:S(2)}, u32[]{:S(2)}) collective-permute-start(f32[2,4,8,320]{3,2,1,0:T(8,128)S(1)} %get-tuple-element.250), channel_id=1, source_target_pairs={{0,4},{4,8},{8,12},{1,5},{5,9},{9,13},{2,6},{6,10},{10,14},{3,7},{... | collective-permute-start | bytes 245768 | tf_op jit(solution)/shard_map/ppermute | solution.py:14
  9.7 9.4 %all-reduce.20 = s32[1024]{0:T(1024)S(1)} all-reduce(s32[1024]{0:T(1024)S(1)} %bitcast_dynamic-update-slice_fusion), channel_id=1, replica_groups=mesh['shot'=2,'gx'=4,'gy'=4] {'gx','gy'}, use_global_device_ids=true, to_apply=%add.20 | all-reduce | flops 1024 | bytes 8192
  23.8 15.2 %all-gather = f32[16,64,10]{1,2,0:T(8,128)S(1)} all-gather(f32[1,64,10]{1,2,0:T(8,128)S(1)} %bitcast.208), channel_id=1, replica_groups=mesh['shot'=2,'gx'=4,'gy'=4] {'gx','gy'}, dimensions={0}, use_global_device_ids=true | all-gather | bytes 43520 | tf_op jit(solution)/shard_map/all_gather | solution.py:68
  39.2 6.0 %scatter_custom_fusion = f32[10,64]{0,1:T(8,128)S(1)} fusion(s32[1024]{0:T(1024)S(1)} %bitcast.209, f32[1024,10]{1,0:T(8,128)S(1)} %bitcast.206, f32[]{:T(128)} %constant.323.clone.1), kind=kCustom, calls=%fused_computation.926 | custom fusion | flops 10240 | bytes 2564 | tf_op jit(solution)/shard_map/scatter-add | solution.py:78
  56.3 4.3 %collective-permute-done.4 = f32[2,4,8,320]{3,2,1,0:T(8,128)S(1)} collective-permute-done((f32[2,4,8,320]{3,2,1,0:T(8,128)S(1)}, f32[2,4,8,320]{3,2,1,0:T(8,128)S(1)}, u32[]{:S(2)}, u32[]{:S(2)}) %collective-permute-start.4) | collective-permute-done | bytes 81952 | tf_op jit(solution)/shard_map/ppermute | solution.py:14
  60.7 3.6 %collective-permute-start.7 = (f32[2,16,4,320]{3,1,2,0:T(8,128)S(1)}, f32[2,16,4,320]{3,1,2,0:T(8,128)S(1)}, u32[]{:S(2)}, u32[]{:S(2)}) collective-permute-start(f32[2,16,4,320]{3,1,2,0:T(8,128)S(1)} %copy.731), channel_id=1, source_target_pairs={{1,0},{2,1},{3,2},{5,4},{6,5},{7,6},{9,8},{10,9},{11,10},{13,12},{... | collective-permute-start | bytes 491528 | tf_op jit(solution)/shard_map/ppermute | solution.py:17
  67.6 3.8 %collective-permute-done.6 = f32[2,16,4,320]{3,1,2,0:T(8,128)S(1)} collective-permute-done((f32[2,16,4,320]{3,1,2,0:T(8,128)S(1)}, f32[2,16,4,320]{3,1,2,0:T(8,128)S(1)}, u32[]{:S(2)}, u32[]{:S(2)}) %collective-permute-start.6) | collective-permute-done | bytes 163872 | tf_op jit(solution)/shard_map/ppermute | solution.py:14
  79.6 3.4 %collective-permute-done.8 = f32[2,4,8,320]{3,2,1,0:T(8,128)S(1)} collective-permute-done((f32[2,4,8,320]{3,2,1,0:T(8,128)S(1)}, f32[2,4,8,320]{3,2,1,0:T(8,128)S(1)}, u32[]{:S(2)}, u32[]{:S(2)}) %collective-permute-start.8) | collective-permute-done | bytes 81952 | tf_op jit(solution)/shard_map/ppermute | solution.py:14
  88.2 3.8 %collective-permute-done.10 = f32[2,16,4,320]{3,1,2,0:T(8,128)S(1)} collective-permute-done((f32[2,16,4,320]{3,1,2,0:T(8,128)S(1)}, f32[2,16,4,320]{3,1,2,0:T(8,128)S(1)}, u32[]{:S(2)}, u32[]{:S(2)}) %collective-permute-start.10) | collective-permute-done | bytes 163872 | tf_op jit(solution)/shard_map/ppermute | solution.py:14
  95.7 3.9 %collective-permute-start.12 = (f32[2,4,8,320]{3,2,1,0:T(8,128)S(1)}, f32[2,4,8,320]{3,2,1,0:T(8,128)S(1)}, u32[]{:S(2)}, u32[]{:S(2)}) collective-permute-start(f32[2,4,8,320]{3,2,1,0:T(8,128)S(1)} %get-tuple-element.244), channel_id=1, source_target_pairs={{0,4},{4,8},{8,12},{1,5},{5,9},{9,13},{2,6},{6,10},{10,14},{3,7},{... | collective-permute-start | bytes 245768 | tf_op jit(solution)/shard_map/ppermute | solution.py:14
  107.5 3.8 %collective-permute-done.14 = f32[2,16,4,320]{3,1,2,0:T(8,128)S(1)} collective-permute-done((f32[2,16,4,320]{3,1,2,0:T(8,128)S(1)}, f32[2,16,4,320]{3,1,2,0:T(8,128)S(1)}, u32[]{:S(2)}, u32[]{:S(2)}) %collective-permute-start.14) | collective-permute-done | bytes 163872 | tf_op jit(solution)/shard_map/ppermute | solution.py:14
  114.9 3.9 %collective-permute-start.16 = (f32[2,4,8,320]{3,2,1,0:T(8,128)S(1)}, f32[2,4,8,320]{3,2,1,0:T(8,128)S(1)}, u32[]{:S(2)}, u32[]{:S(2)}) collective-permute-start(f32[2,4,8,320]{3,2,1,0:T(8,128)S(1)} %get-tuple-element.242), channel_id=1, source_target_pairs={{0,4},{4,8},{8,12},{1,5},{5,9},{9,13},{2,6},{6,10},{10,14},{3,7},{... | collective-permute-start | bytes 245768 | tf_op jit(solution)/shard_map/ppermute | solution.py:14
  126.7 3.8 %collective-permute-done.18 = f32[2,16,4,320]{3,1,2,0:T(8,128)S(1)} collective-permute-done((f32[2,16,4,320]{3,1,2,0:T(8,128)S(1)}, f32[2,16,4,320]{3,1,2,0:T(8,128)S(1)}, u32[]{:S(2)}, u32[]{:S(2)}) %collective-permute-start.18) | collective-permute-done | bytes 163872 | tf_op jit(solution)/shard_map/ppermute | solution.py:14
  134.2 3.9 %collective-permute-start.20 = (f32[2,4,8,320]{3,2,1,0:T(8,128)S(1)}, f32[2,4,8,320]{3,2,1,0:T(8,128)S(1)}, u32[]{:S(2)}, u32[]{:S(2)}) collective-permute-start(f32[2,4,8,320]{3,2,1,0:T(8,128)S(1)} %get-tuple-element.240), channel_id=1, source_target_pairs={{0,4},{4,8},{8,12},{1,5},{5,9},{9,13},{2,6},{6,10},{10,14},{3,7},{... | collective-permute-start | bytes 245768 | tf_op jit(solution)/shard_map/ppermute | solution.py:14
  146.0 3.8 %collective-permute-done.22 = f32[2,16,4,320]{3,1,2,0:T(8,128)S(1)} collective-permute-done((f32[2,16,4,320]{3,1,2,0:T(8,128)S(1)}, f32[2,16,4,320]{3,1,2,0:T(8,128)S(1)}, u32[]{:S(2)}, u32[]{:S(2)}) %collective-permute-start.22) | collective-permute-done | bytes 163872 | tf_op jit(solution)/shard_map/ppermute | solution.py:14
  153.4 3.9 %collective-permute-start.24 = (f32[2,4,8,320]{3,2,1,0:T(8,128)S(1)}, f32[2,4,8,320]{3,2,1,0:T(8,128)S(1)}, u32[]{:S(2)}, u32[]{:S(2)}) collective-permute-start(f32[2,4,8,320]{3,2,1,0:T(8,128)S(1)} %get-tuple-element.238), channel_id=1, source_target_pairs={{0,4},{4,8},{8,12},{1,5},{5,9},{9,13},{2,6},{6,10},{10,14},{3,7},{... | collective-permute-start | bytes 245768 | tf_op jit(solution)/shard_map/ppermute | solution.py:14
  165.2 3.8 %collective-permute-done.26 = f32[2,16,4,320]{3,1,2,0:T(8,128)S(1)} collective-permute-done((f32[2,16,4,320]{3,1,2,0:T(8,128)S(1)}, f32[2,16,4,320]{3,1,2,0:T(8,128)S(1)}, u32[]{:S(2)}, u32[]{:S(2)}) %collective-permute-start.26) | collective-permute-done | bytes 163872 | tf_op jit(solution)/shard_map/ppermute | solution.py:14
  172.7 3.9 %collective-permute-start.28 = (f32[2,4,8,320]{3,2,1,0:T(8,128)S(1)}, f32[2,4,8,320]{3,2,1,0:T(8,128)S(1)}, u32[]{:S(2)}, u32[]{:S(2)}) collective-permute-start(f32[2,4,8,320]{3,2,1,0:T(8,128)S(1)} %get-tuple-element.236), channel_id=1, source_target_pairs={{0,4},{4,8},{8,12},{1,5},{5,9},{9,13},{2,6},{6,10},{10,14},{3,7},{... | collective-permute-start | bytes 245768 | tf_op jit(solution)/shard_map/ppermute | solution.py:14
  184.5 3.8 %collective-permute-done.30 = f32[2,16,4,320]{3,1,2,0:T(8,128)S(1)} collective-permute-done((f32[2,16,4,320]{3,1,2,0:T(8,128)S(1)}, f32[2,16,4,320]{3,1,2,0:T(8,128)S(1)}, u32[]{:S(2)}, u32[]{:S(2)}) %collective-permute-start.30) | collective-permute-done | bytes 163872 | tf_op jit(solution)/shard_map/ppermute | solution.py:14
  191.9 3.9 %collective-permute-start.32 = (f32[2,4,8,320]{3,2,1,0:T(8,128)S(1)}, f32[2,4,8,320]{3,2,1,0:T(8,128)S(1)}, u32[]{:S(2)}, u32[]{:S(2)}) collective-permute-start(f32[2,4,8,320]{3,2,1,0:T(8,128)S(1)} %get-tuple-element.234), channel_id=1, source_target_pairs={{0,4},{4,8},{8,12},{1,5},{5,9},{9,13},{2,6},{6,10},{10,14},{3,7},{... | collective-permute-start | bytes 245768 | tf_op jit(solution)/shard_map/ppermute | solution.py:14
  203.8 3.8 %collective-permute-done.34 = f32[2,16,4,320]{3,1,2,0:T(8,128)S(1)} collective-permute-done((f32[2,16,4,320]{3,1,2,0:T(8,128)S(1)}, f32[2,16,4,320]{3,1,2,0:T(8,128)S(1)}, u32[]{:S(2)}, u32[]{:S(2)}) %collective-permute-start.34) | collective-permute-done | bytes 163872 | tf_op jit(solution)/shard_map/ppermute | solution.py:14
  211.4 3.9 %collective-permute-start.36 = (f32[2,4,8,320]{3,2,1,0:T(8,128)S(1)}, f32[2,4,8,320]{3,2,1,0:T(8,128)S(1)}, u32[]{:S(2)}, u32[]{:S(2)}) collective-permute-start(f32[2,4,8,320]{3,2,1,0:T(8,128)S(1)} %get-tuple-element.232), channel_id=1, source_target_pairs={{0,4},{4,8},{8,12},{1,5},{5,9},{9,13},{2,6},{6,10},{10,14},{3,7},{... | collective-permute-start | bytes 245768 | tf_op jit(solution)/shard_map/ppermute | solution.py:14
  240.4 3.7 %collective-permute-done.38 = f32[2,16,4,320]{3,1,2,0:T(8,128)S(1)} collective-permute-done((f32[2,16,4,320]{3,1,2,0:T(8,128)S(1)}, f32[2,16,4,320]{3,1,2,0:T(8,128)S(1)}, u32[]{:S(2)}, u32[]{:S(2)}) %collective-permute-start.38) | collective-permute-done | bytes 163872 | tf_op jit(solution)/shard_map/ppermute | solution.py:14
  247.3 7.1 %fusion.361 = (f32[8,8,320]{2,1,0:T(8,128)}, f32[8,8,320]{2,1,0:T(8,128)}) fusion(f32[8,8,320]{2,1,0:T(8,128)S(1)} %multiply_add_fusion.1, f32[8,8,320]{2,1,0:T(8,128)S(1)} %multiply_add_fusion.3, f32[8,8,320]{2,1,0:T(8,128)S(1)} %multiply_add_fusion.4, f32[8,8,320]{2,1,0:T(8,128)S(1)} %multiply_add_fusion.8, f32[8,8,320]{2,1,0:T(8,128)S(1)} %copy-done.7, ...), kind=kLoop, calls=%fused_computation.864 | loop fusion | flops 1228800 | bytes 1556530 | tf_op jit(solution)/shard_map/add | solution.py:116
  (239 shorter events, 118.4 us)
Async XLA Ops:
  1.6 17.6 %collective-permute-start.1 = (f32[2,4,8,320]{3,2,1,0:T(8,128)S(1)}, f32[2,4,8,320]{3,2,1,0:T(8,128)S(1)}, u32[]{:S(2)}, u32[]{:S(2)}) collective-permute-start(f32[2,4,8,320]{3,2,1,0:T(8,128)S(1)} %get-tuple-element.251), channel_id=1, source_target_pairs={{4,0},{8,4},{12,8},{5,1},{9,5},{13,9},{6,2},{10,6},{14,10},{7,3},{... | collective-permute-start | bytes 245768 | tf_op jit(solution)/shard_map/ppermute | solution.py:17
  4.1 15.1 %collective-permute-start = (f32[2,4,8,320]{3,2,1,0:T(8,128)S(1)}, f32[2,4,8,320]{3,2,1,0:T(8,128)S(1)}, u32[]{:S(2)}, u32[]{:S(2)}) collective-permute-start(f32[2,4,8,320]{3,2,1,0:T(8,128)S(1)} %get-tuple-element.250), channel_id=1, source_target_pairs={{0,4},{4,8},{8,12},{1,5},{5,9},{9,13},{2,6},{6,10},{10,14},{3,7},{... | collective-permute-start | bytes 245768 | tf_op jit(solution)/shard_map/ppermute | solution.py:14
  19.3 26.6 %collective-permute-start.3 = (f32[2,16,4,320]{3,1,2,0:T(8,128)S(1)}, f32[2,16,4,320]{3,1,2,0:T(8,128)S(1)}, u32[]{:S(2)}, u32[]{:S(2)}) collective-permute-start(f32[2,16,4,320]{3,1,2,0:T(8,128)S(1)} %copy.729), channel_id=1, source_target_pairs={{1,0},{2,1},{3,2},{5,4},{6,5},{7,6},{9,8},{10,9},{11,10},{13,12},{... | collective-permute-start | bytes 491528 | tf_op jit(solution)/shard_map/ppermute | solution.py:17
  21.3 24.7 %collective-permute-start.2 = (f32[2,16,4,320]{3,1,2,0:T(8,128)S(1)}, f32[2,16,4,320]{3,1,2,0:T(8,128)S(1)}, u32[]{:S(2)}, u32[]{:S(2)}) collective-permute-start(f32[2,16,4,320]{3,1,2,0:T(8,128)S(1)} %copy.728), channel_id=1, source_target_pairs={{0,1},{1,2},{2,3},{4,5},{5,6},{6,7},{8,9},{9,10},{10,11},{12,13},{... | collective-permute-start | bytes 491528 | tf_op jit(solution)/shard_map/ppermute | solution.py:14
  49.3 6.9 %collective-permute-start.5 = (f32[2,4,8,320]{3,2,1,0:T(8,128)S(1)}, f32[2,4,8,320]{3,2,1,0:T(8,128)S(1)}, u32[]{:S(2)}, u32[]{:S(2)}) collective-permute-start(f32[2,4,8,320]{3,2,1,0:T(8,128)S(1)} %get-tuple-element.249), channel_id=1, source_target_pairs={{4,0},{8,4},{12,8},{5,1},{9,5},{13,9},{6,2},{10,6},{14,10},{7,3},{... | collective-permute-start | bytes 245768 | tf_op jit(solution)/shard_map/ppermute | solution.py:17
  52.6 8.0 %collective-permute-start.4 = (f32[2,4,8,320]{3,2,1,0:T(8,128)S(1)}, f32[2,4,8,320]{3,2,1,0:T(8,128)S(1)}, u32[]{:S(2)}, u32[]{:S(2)}) collective-permute-start(f32[2,4,8,320]{3,2,1,0:T(8,128)S(1)} %get-tuple-element.248), channel_id=1, source_target_pairs={{0,4},{4,8},{8,12},{1,5},{5,9},{9,13},{2,6},{6,10},{10,14},{3,7},{... | collective-permute-start | bytes 245768 | tf_op jit(solution)/shard_map/ppermute | solution.py:14
  60.7 6.8 %collective-permute-start.7 = (f32[2,16,4,320]{3,1,2,0:T(8,128)S(1)}, f32[2,16,4,320]{3,1,2,0:T(8,128)S(1)}, u32[]{:S(2)}, u32[]{:S(2)}) collective-permute-start(f32[2,16,4,320]{3,1,2,0:T(8,128)S(1)} %copy.731), channel_id=1, source_target_pairs={{1,0},{2,1},{3,2},{5,4},{6,5},{7,6},{9,8},{10,9},{11,10},{13,12},{... | collective-permute-start | bytes 491528 | tf_op jit(solution)/shard_map/ppermute | solution.py:17
  64.4 7.0 %collective-permute-start.6 = (f32[2,16,4,320]{3,1,2,0:T(8,128)S(1)}, f32[2,16,4,320]{3,1,2,0:T(8,128)S(1)}, u32[]{:S(2)}, u32[]{:S(2)}) collective-permute-start(f32[2,16,4,320]{3,1,2,0:T(8,128)S(1)} %copy.730), channel_id=1, source_target_pairs={{0,1},{1,2},{2,3},{4,5},{5,6},{6,7},{8,9},{9,10},{10,11},{12,13},{... | collective-permute-start | bytes 491528 | tf_op jit(solution)/shard_map/ppermute | solution.py:14
  73.1 6.5 %collective-permute-start.9 = (f32[2,4,8,320]{3,2,1,0:T(8,128)S(1)}, f32[2,4,8,320]{3,2,1,0:T(8,128)S(1)}, u32[]{:S(2)}, u32[]{:S(2)}) collective-permute-start(f32[2,4,8,320]{3,2,1,0:T(8,128)S(1)} %get-tuple-element.247), channel_id=1, source_target_pairs={{4,0},{8,4},{12,8},{5,1},{9,5},{13,9},{6,2},{10,6},{14,10},{7,3},{... | collective-permute-start | bytes 245768 | tf_op jit(solution)/shard_map/ppermute | solution.py:17
  76.4 6.5 %collective-permute-start.8 = (f32[2,4,8,320]{3,2,1,0:T(8,128)S(1)}, f32[2,4,8,320]{3,2,1,0:T(8,128)S(1)}, u32[]{:S(2)}, u32[]{:S(2)}) collective-permute-start(f32[2,4,8,320]{3,2,1,0:T(8,128)S(1)} %get-tuple-element.246), channel_id=1, source_target_pairs={{0,4},{4,8},{8,12},{1,5},{5,9},{9,13},{2,6},{6,10},{10,14},{3,7},{... | collective-permute-start | bytes 245768 | tf_op jit(solution)/shard_map/ppermute | solution.py:14
  85.0 7.0 %collective-permute-start.10 = (f32[2,16,4,320]{3,1,2,0:T(8,128)S(1)}, f32[2,16,4,320]{3,1,2,0:T(8,128)S(1)}, u32[]{:S(2)}, u32[]{:S(2)}) collective-permute-start(f32[2,16,4,320]{3,1,2,0:T(8,128)S(1)} %copy.732), channel_id=1, source_target_pairs={{0,1},{1,2},{2,3},{4,5},{5,6},{6,7},{8,9},{9,10},{10,11},{12,13},{... | collective-permute-start | bytes 491528 | tf_op jit(solution)/shard_map/ppermute | solution.py:14
  93.7 6.5 %collective-permute-start.13 = (f32[2,4,8,320]{3,2,1,0:T(8,128)S(1)}, f32[2,4,8,320]{3,2,1,0:T(8,128)S(1)}, u32[]{:S(2)}, u32[]{:S(2)}) collective-permute-start(f32[2,4,8,320]{3,2,1,0:T(8,128)S(1)} %get-tuple-element.245), channel_id=1, source_target_pairs={{4,0},{8,4},{12,8},{5,1},{9,5},{13,9},{6,2},{10,6},{14,10},{7,3},{... | collective-permute-start | bytes 245768 | tf_op jit(solution)/shard_map/ppermute | solution.py:17
  95.7 6.5 %collective-permute-start.12 = (f32[2,4,8,320]{3,2,1,0:T(8,128)S(1)}, f32[2,4,8,320]{3,2,1,0:T(8,128)S(1)}, u32[]{:S(2)}, u32[]{:S(2)}) collective-permute-start(f32[2,4,8,320]{3,2,1,0:T(8,128)S(1)} %get-tuple-element.244), channel_id=1, source_target_pairs={{0,4},{4,8},{8,12},{1,5},{5,9},{9,13},{2,6},{6,10},{10,14},{3,7},{... | collective-permute-start | bytes 245768 | tf_op jit(solution)/shard_map/ppermute | solution.py:14
  104.2 7.0 %collective-permute-start.14 = (f32[2,16,4,320]{3,1,2,0:T(8,128)S(1)}, f32[2,16,4,320]{3,1,2,0:T(8,128)S(1)}, u32[]{:S(2)}, u32[]{:S(2)}) collective-permute-start(f32[2,16,4,320]{3,1,2,0:T(8,128)S(1)} %copy.734), channel_id=1, source_target_pairs={{0,1},{1,2},{2,3},{4,5},{5,6},{6,7},{8,9},{9,10},{10,11},{12,13},{... | collective-permute-start | bytes 491528 | tf_op jit(solution)/shard_map/ppermute | solution.py:14
  113.0 6.5 %collective-permute-start.17 = (f32[2,4,8,320]{3,2,1,0:T(8,128)S(1)}, f32[2,4,8,320]{3,2,1,0:T(8,128)S(1)}, u32[]{:S(2)}, u32[]{:S(2)}) collective-permute-start(f32[2,4,8,320]{3,2,1,0:T(8,128)S(1)} %get-tuple-element.243), channel_id=1, source_target_pairs={{4,0},{8,4},{12,8},{5,1},{9,5},{13,9},{6,2},{10,6},{14,10},{7,3},{... | collective-permute-start | bytes 245768 | tf_op jit(solution)/shard_map/ppermute | solution.py:17
  114.9 6.5 %collective-permute-start.16 = (f32[2,4,8,320]{3,2,1,0:T(8,128)S(1)}, f32[2,4,8,320]{3,2,1,0:T(8,128)S(1)}, u32[]{:S(2)}, u32[]{:S(2)}) collective-permute-start(f32[2,4,8,320]{3,2,1,0:T(8,128)S(1)} %get-tuple-element.242), channel_id=1, source_target_pairs={{0,4},{4,8},{8,12},{1,5},{5,9},{9,13},{2,6},{6,10},{10,14},{3,7},{... | collective-permute-start | bytes 245768 | tf_op jit(solution)/shard_map/ppermute | solution.py:14
  123.5 7.0 %collective-permute-start.18 = (f32[2,16,4,320]{3,1,2,0:T(8,128)S(1)}, f32[2,16,4,320]{3,1,2,0:T(8,128)S(1)}, u32[]{:S(2)}, u32[]{:S(2)}) collective-permute-start(f32[2,16,4,320]{3,1,2,0:T(8,128)S(1)} %copy.736), channel_id=1, source_target_pairs={{0,1},{1,2},{2,3},{4,5},{5,6},{6,7},{8,9},{9,10},{10,11},{12,13},{... | collective-permute-start | bytes 491528 | tf_op jit(solution)/shard_map/ppermute | solution.py:14
  142.7 7.0 %collective-permute-start.22 = (f32[2,16,4,320]{3,1,2,0:T(8,128)S(1)}, f32[2,16,4,320]{3,1,2,0:T(8,128)S(1)}, u32[]{:S(2)}, u32[]{:S(2)}) collective-permute-start(f32[2,16,4,320]{3,1,2,0:T(8,128)S(1)} %copy.738), channel_id=1, source_target_pairs={{0,1},{1,2},{2,3},{4,5},{5,6},{6,7},{8,9},{9,10},{10,11},{12,13},{... | collective-permute-start | bytes 491528 | tf_op jit(solution)/shard_map/ppermute | solution.py:14
  162.0 7.0 %collective-permute-start.26 = (f32[2,16,4,320]{3,1,2,0:T(8,128)S(1)}, f32[2,16,4,320]{3,1,2,0:T(8,128)S(1)}, u32[]{:S(2)}, u32[]{:S(2)}) collective-permute-start(f32[2,16,4,320]{3,1,2,0:T(8,128)S(1)} %copy.740), channel_id=1, source_target_pairs={{0,1},{1,2},{2,3},{4,5},{5,6},{6,7},{8,9},{9,10},{10,11},{12,13},{... | collective-permute-start | bytes 491528 | tf_op jit(solution)/shard_map/ppermute | solution.py:14
  181.3 7.0 %collective-permute-start.30 = (f32[2,16,4,320]{3,1,2,0:T(8,128)S(1)}, f32[2,16,4,320]{3,1,2,0:T(8,128)S(1)}, u32[]{:S(2)}, u32[]{:S(2)}) collective-permute-start(f32[2,16,4,320]{3,1,2,0:T(8,128)S(1)} %copy.742), channel_id=1, source_target_pairs={{0,1},{1,2},{2,3},{4,5},{5,6},{6,7},{8,9},{9,10},{10,11},{12,13},{... | collective-permute-start | bytes 491528 | tf_op jit(solution)/shard_map/ppermute | solution.py:14
  200.5 7.0 %collective-permute-start.34 = (f32[2,16,4,320]{3,1,2,0:T(8,128)S(1)}, f32[2,16,4,320]{3,1,2,0:T(8,128)S(1)}, u32[]{:S(2)}, u32[]{:S(2)}) collective-permute-start(f32[2,16,4,320]{3,1,2,0:T(8,128)S(1)} %copy.744), channel_id=1, source_target_pairs={{0,1},{1,2},{2,3},{4,5},{5,6},{6,7},{8,9},{9,10},{10,11},{12,13},{... | collective-permute-start | bytes 491528 | tf_op jit(solution)/shard_map/ppermute | solution.py:14
  209.3 25.6 %collective-permute-start.37 = (f32[2,4,8,320]{3,2,1,0:T(8,128)S(1)}, f32[2,4,8,320]{3,2,1,0:T(8,128)S(1)}, u32[]{:S(2)}, u32[]{:S(2)}) collective-permute-start(f32[2,4,8,320]{3,2,1,0:T(8,128)S(1)} %get-tuple-element.233), channel_id=1, source_target_pairs={{4,0},{8,4},{12,8},{5,1},{9,5},{13,9},{6,2},{10,6},{14,10},{7,3},{... | collective-permute-start | bytes 245768 | tf_op jit(solution)/shard_map/ppermute | solution.py:17
  211.4 23.6 %collective-permute-start.36 = (f32[2,4,8,320]{3,2,1,0:T(8,128)S(1)}, f32[2,4,8,320]{3,2,1,0:T(8,128)S(1)}, u32[]{:S(2)}, u32[]{:S(2)}) collective-permute-start(f32[2,4,8,320]{3,2,1,0:T(8,128)S(1)} %get-tuple-element.232), channel_id=1, source_target_pairs={{0,4},{4,8},{8,12},{1,5},{5,9},{9,13},{2,6},{6,10},{10,14},{3,7},{... | collective-permute-start | bytes 245768 | tf_op jit(solution)/shard_map/ppermute | solution.py:14
  237.1 7.0 %collective-permute-start.38 = (f32[2,16,4,320]{3,1,2,0:T(8,128)S(1)}, f32[2,16,4,320]{3,1,2,0:T(8,128)S(1)}, u32[]{:S(2)}, u32[]{:S(2)}) collective-permute-start(f32[2,16,4,320]{3,1,2,0:T(8,128)S(1)} %copy.746), channel_id=1, source_target_pairs={{0,1},{1,2},{2,3},{4,5},{5,6},{6,7},{8,9},{9,10},{10,11},{12,13},{... | collective-permute-start | bytes 491528 | tf_op jit(solution)/shard_map/ppermute | solution.py:14
  (30 other events, 239.4 us)
where the time goes:
time: 256 us; the launch traced here: 254 us
  starting transfers between devices  103 us (40%)
  waiting for transfers between devices  64.8 us (25%)
  other arithmetic  32.2 us (13%)
  blocking collectives  24.6 us (10%)
  between operations  22.2 us (9%)
  local copies, waits for them, and re-layouts  7.13 us (3%)
    ppermute x20, starting transfers between devices, with_halo(): lax.ppermute(lax.slice_in_dim(block, block.shape[dim] - width, None, axis...  59.8 us
    ppermute x20, waiting for transfers between devices, with_halo(): lax.ppermute(lax.slice_in_dim(block, block.shape[dim] - width, None, axis...  53 us
    ppermute x20, starting transfers between devices, with_halo(): lax.ppermute(lax.slice_in_dim(block, 0, width, axis=dim), axis, backward)  43.6 us
    all_gather x1, blocking collectives, body(): values = lax.all_gather(traces, ('gx', 'gy'), axis=1, tiled=True)  15.2 us
    ppermute x20, waiting for transfers between devices, with_halo(): lax.ppermute(lax.slice_in_dim(block, 0, width, axis=dim), axis, backward)  11.7 us
    convert_element_type x10, other arithmetic, body(): source_field.astype(jnp.bfloat16)[None]  9.89 us
    unnamed x1, blocking collectives  9.37 us
    add x1, other arithmetic, body(): imaged = imaged + jnp.where(present, snapshot * receiver_field, 0.0)  7.05 us
  transfers between devices with their start and end apart: 40, of which 33 were waited for; matrix products, arithmetic and copies ran while one was open for 4% of the time, Pallas kernels for 0%

commit v1 on v0

--- a/solution.py
+++ b/solution.py
@@ -65,7 +65,10 @@
     span_x = block_x + 2 * border
     span_y = block_y + 2 * border
     plane_cells = span_x * span_y
-    values = lax.all_gather(traces, ("gx", "gy"), axis=1, tiled=True)
+    values = jnp.concatenate(
+        lax.all_to_all(jnp.stack([traces] * lax.axis_size(("gx", "gy"))), ("gx", "gy"), 0, 0),
+        axis=1,
+    )
     cell_ids = lax.all_gather(receiver_cells, ("gx", "gy"), axis=1, tiled=True)
     cell_ids = cell_ids[0]
     local_x = cell_ids // grid_y - (start_x - border)

time: 256 us -> 246 us (0.961)
  blocking collectives: 24.6 us -> 9.48 us
  starting transfers between devices: 103 us -> 107 us
    all_gather x1 -> x0, blocking collectives: 15.2 us -> none  [body(): values = lax.all_gather(traces, ('gx', 'gy'), axis=1, tiled=True)]
    all_to_all x0 -> x1, starting transfers between devices: none -> 5.25 us  [body(): lax.all_to_all(jnp.stack([traces] * lax.axis_size(('gx', 'gy'))), ('gx',...]
  transfers between devices with their start and end apart: 40 -> 41, of which waited for: 33 -> 33; matrix products, arithmetic and copies ran while one was open for 4% -> 5% of each run, Pallas kernels for 0% -> 0%
where the time goes in v1:
time: 246 us; the launch traced here: 244 us
  starting transfers between devices  107 us (43%)
  waiting for transfers between devices  63.4 us (26%)
  other arithmetic  32.9 us (13%)
  between operations  22.1 us (9%)
  blocking collectives  9.48 us (4%)
  local copies, waits for them, and re-layouts  8.56 us (3%)
    ppermute x20, starting transfers between devices, with_halo(): lax.ppermute(lax.slice_in_dim(block, block.shape[dim] - width, None, axis...  59.8 us
    ppermute x20, waiting for transfers between devices, with_halo(): lax.ppermute(lax.slice_in_dim(block, block.shape[dim] - width, None, axis...  52.2 us
    ppermute x20, starting transfers between devices, with_halo(): lax.ppermute(lax.slice_in_dim(block, 0, width, axis=dim), axis, backward)  42.3 us
    ppermute x20, waiting for transfers between devices, with_halo(): lax.ppermute(lax.slice_in_dim(block, 0, width, axis=dim), axis, backward)  11.1 us
    convert_element_type x10, other arithmetic, body(): source_field.astype(jnp.bfloat16)[None]  9.81 us
    unnamed x1, blocking collectives  9.48 us
    add x1, other arithmetic, body(): imaged = imaged + jnp.where(present, snapshot * receiver_field, 0.0)  7.04 us
    scatter-add x1, other arithmetic, body(): injected = jnp.zeros((total_steps, plane_cells), jnp.float32).at[:, local...  6.04 us
  transfers between devices with their start and end apart: 41, of which 33 were waited for; matrix products, arithmetic and copies ran while one was open for 5% of the time, Pallas kernels for 0%

profile of v1, /device:TPU:18, one launch (start us, length us, event | category | flops | bytes accessed | tf_op | source)
XLA Modules:
  0.0 243.7 jit_solution(6953681213085616724)
XLA Ops:
  3.9 3.5 %collective-permute-start = (f32[2,4,8,320]{3,2,1,0:T(8,128)S(1)}, f32[2,4,8,320]{3,2,1,0:T(8,128)S(1)}, u32[]{:S(2)}, u32[]{:S(2)}) collective-permute-start(f32[2,4,8,320]{3,2,1,0:T(8,128)S(1)} %get-tuple-element.256), channel_id=1, source_target_pairs={{0,4},{4,8},{8,12},{1,5},{5,9},{9,13},{2,6},{6,10},{10,14},{3,7},{... | collective-permute-start | bytes 245768 | tf_op jit(solution)/shard_map/ppermute | solution.py:14
  8.2 5.2 %all-to-all-start = ((f32[16,1,640]{2,1,0:T(1,128)}), f32[16,1,640]{2,1,0:T(1,128)S(1)}, u32[]{:S(2)}, u32[]{:S(2)}) async-start(f32[16,1,640]{2,1,0:T(1,128)} %reshape.617), calls=%async_computation | async-start | bytes 81920 | tf_op jit(solution)/shard_map/all_to_all | solution.py:69
  15.5 9.5 %all-reduce.20 = s32[1024]{0:T(1024)S(1)} all-reduce(s32[1024]{0:T(1024)S(1)} %bitcast_dynamic-update-slice_fusion), channel_id=1, replica_groups=mesh['shot'=2,'gx'=4,'gy'=4] {'gx','gy'}, use_global_device_ids=true, to_apply=%add.20 | all-reduce | flops 1024 | bytes 8192
  32.1 6.0 %scatter_custom_fusion = f32[10,64]{0,1:T(8,128)S(1)} fusion(s32[1024]{0:T(1024)S(1)} %bitcast.207, f32[1024,10]{1,0:T(8,128)S(1)} %copy.882, f32[]{:T(128)} %constant.323.clone.1), kind=kCustom, calls=%fused_computation.926 | custom fusion | flops 10240 | bytes 2564 | tf_op jit(solution)/shard_map/scatter-add | solution.py:81
  48.0 3.4 %collective-permute-done.4 = f32[2,4,8,320]{3,2,1,0:T(8,128)S(1)} collective-permute-done((f32[2,4,8,320]{3,2,1,0:T(8,128)S(1)}, f32[2,4,8,320]{3,2,1,0:T(8,128)S(1)}, u32[]{:S(2)}, u32[]{:S(2)}) %collective-permute-start.4) | collective-permute-done | bytes 81952 | tf_op jit(solution)/shard_map/ppermute | solution.py:14
  57.0 3.8 %collective-permute-done.6 = f32[2,16,4,320]{3,1,2,0:T(8,128)S(1)} collective-permute-done((f32[2,16,4,320]{3,1,2,0:T(8,128)S(1)}, f32[2,16,4,320]{3,1,2,0:T(8,128)S(1)}, u32[]{:S(2)}, u32[]{:S(2)}) %collective-permute-start.6) | collective-permute-done | bytes 163872 | tf_op jit(solution)/shard_map/ppermute | solution.py:14
  62.5 3.5 %collective-permute-start.9 = (f32[2,4,8,320]{3,2,1,0:T(8,128)S(1)}, f32[2,4,8,320]{3,2,1,0:T(8,128)S(1)}, u32[]{:S(2)}, u32[]{:S(2)}) collective-permute-start(f32[2,4,8,320]{3,2,1,0:T(8,128)S(1)} %get-tuple-element.253), channel_id=1, source_target_pairs={{4,0},{8,4},{12,8},{5,1},{9,5},{13,9},{6,2},{10,6},{14,10},{7,3},{... | collective-permute-start | bytes 245768 | tf_op jit(solution)/shard_map/ppermute | solution.py:17
  69.0 3.5 %collective-permute-done.8 = f32[2,4,8,320]{3,2,1,0:T(8,128)S(1)} collective-permute-done((f32[2,4,8,320]{3,2,1,0:T(8,128)S(1)}, f32[2,4,8,320]{3,2,1,0:T(8,128)S(1)}, u32[]{:S(2)}, u32[]{:S(2)}) %collective-permute-start.8) | collective-permute-done | bytes 81952 | tf_op jit(solution)/shard_map/ppermute | solution.py:14
  77.8 3.8 %collective-permute-done.10 = f32[2,16,4,320]{3,1,2,0:T(8,128)S(1)} collective-permute-done((f32[2,16,4,320]{3,1,2,0:T(8,128)S(1)}, f32[2,16,4,320]{3,1,2,0:T(8,128)S(1)}, u32[]{:S(2)}, u32[]{:S(2)}) %collective-permute-start.10) | collective-permute-done | bytes 163872 | tf_op jit(solution)/shard_map/ppermute | solution.py:14
  85.2 3.9 %collective-permute-start.12 = (f32[2,4,8,320]{3,2,1,0:T(8,128)S(1)}, f32[2,4,8,320]{3,2,1,0:T(8,128)S(1)}, u32[]{:S(2)}, u32[]{:S(2)}) collective-permute-start(f32[2,4,8,320]{3,2,1,0:T(8,128)S(1)} %get-tuple-element.250), channel_id=1, source_target_pairs={{0,4},{4,8},{8,12},{1,5},{5,9},{9,13},{2,6},{6,10},{10,14},{3,7},{... | collective-permute-start | bytes 245768 | tf_op jit(solution)/shard_map/ppermute | solution.py:14
  97.0 3.8 %collective-permute-done.14 = f32[2,16,4,320]{3,1,2,0:T(8,128)S(1)} collective-permute-done((f32[2,16,4,320]{3,1,2,0:T(8,128)S(1)}, f32[2,16,4,320]{3,1,2,0:T(8,128)S(1)}, u32[]{:S(2)}, u32[]{:S(2)}) %collective-permute-start.14) | collective-permute-done | bytes 163872 | tf_op jit(solution)/shard_map/ppermute | solution.py:14
  104.4 3.9 %collective-permute-start.16 = (f32[2,4,8,320]{3,2,1,0:T(8,128)S(1)}, f32[2,4,8,320]{3,2,1,0:T(8,128)S(1)}, u32[]{:S(2)}, u32[]{:S(2)}) collective-permute-start(f32[2,4,8,320]{3,2,1,0:T(8,128)S(1)} %get-tuple-element.248), channel_id=1, source_target_pairs={{0,4},{4,8},{8,12},{1,5},{5,9},{9,13},{2,6},{6,10},{10,14},{3,7},{... | collective-permute-start | bytes 245768 | tf_op jit(solution)/shard_map/ppermute | solution.py:14
  116.2 3.8 %collective-permute-done.18 = f32[2,16,4,320]{3,1,2,0:T(8,128)S(1)} collective-permute-done((f32[2,16,4,320]{3,1,2,0:T(8,128)S(1)}, f32[2,16,4,320]{3,1,2,0:T(8,128)S(1)}, u32[]{:S(2)}, u32[]{:S(2)}) %collective-permute-start.18) | collective-permute-done | bytes 163872 | tf_op jit(solution)/shard_map/ppermute | solution.py:14
  123.6 3.9 %collective-permute-start.20 = (f32[2,4,8,320]{3,2,1,0:T(8,128)S(1)}, f32[2,4,8,320]{3,2,1,0:T(8,128)S(1)}, u32[]{:S(2)}, u32[]{:S(2)}) collective-permute-start(f32[2,4,8,320]{3,2,1,0:T(8,128)S(1)} %get-tuple-element.246), channel_id=1, source_target_pairs={{0,4},{4,8},{8,12},{1,5},{5,9},{9,13},{2,6},{6,10},{10,14},{3,7},{... | collective-permute-start | bytes 245768 | tf_op jit(solution)/shard_map/ppermute | solution.py:14
  135.4 3.8 %collective-permute-done.22 = f32[2,16,4,320]{3,1,2,0:T(8,128)S(1)} collective-permute-done((f32[2,16,4,320]{3,1,2,0:T(8,128)S(1)}, f32[2,16,4,320]{3,1,2,0:T(8,128)S(1)}, u32[]{:S(2)}, u32[]{:S(2)}) %collective-permute-start.22) | collective-permute-done | bytes 163872 | tf_op jit(solution)/shard_map/ppermute | solution.py:14
  142.9 3.9 %collective-permute-start.24 = (f32[2,4,8,320]{3,2,1,0:T(8,128)S(1)}, f32[2,4,8,320]{3,2,1,0:T(8,128)S(1)}, u32[]{:S(2)}, u32[]{:S(2)}) collective-permute-start(f32[2,4,8,320]{3,2,1,0:T(8,128)S(1)} %get-tuple-element.244), channel_id=1, source_target_pairs={{0,4},{4,8},{8,12},{1,5},{5,9},{9,13},{2,6},{6,10},{10,14},{3,7},{... | collective-permute-start | bytes 245768 | tf_op jit(solution)/shard_map/ppermute | solution.py:14
  154.7 3.8 %collective-permute-done.26 = f32[2,16,4,320]{3,1,2,0:T(8,128)S(1)} collective-permute-done((f32[2,16,4,320]{3,1,2,0:T(8,128)S(1)}, f32[2,16,4,320]{3,1,2,0:T(8,128)S(1)}, u32[]{:S(2)}, u32[]{:S(2)}) %collective-permute-start.26) | collective-permute-done | bytes 163872 | tf_op jit(solution)/shard_map/ppermute | solution.py:14
  162.2 3.9 %collective-permute-start.28 = (f32[2,4,8,320]{3,2,1,0:T(8,128)S(1)}, f32[2,4,8,320]{3,2,1,0:T(8,128)S(1)}, u32[]{:S(2)}, u32[]{:S(2)}) collective-permute-start(f32[2,4,8,320]{3,2,1,0:T(8,128)S(1)} %get-tuple-element.242), channel_id=1, source_target_pairs={{0,4},{4,8},{8,12},{1,5},{5,9},{9,13},{2,6},{6,10},{10,14},{3,7},{... | collective-permute-start | bytes 245768 | tf_op jit(solution)/shard_map/ppermute | solution.py:14
  174.0 3.8 %collective-permute-done.30 = f32[2,16,4,320]{3,1,2,0:T(8,128)S(1)} collective-permute-done((f32[2,16,4,320]{3,1,2,0:T(8,128)S(1)}, f32[2,16,4,320]{3,1,2,0:T(8,128)S(1)}, u32[]{:S(2)}, u32[]{:S(2)}) %collective-permute-start.30) | collective-permute-done | bytes 163872 | tf_op jit(solution)/shard_map/ppermute | solution.py:14
  181.4 3.9 %collective-permute-start.32 = (f32[2,4,8,320]{3,2,1,0:T(8,128)S(1)}, f32[2,4,8,320]{3,2,1,0:T(8,128)S(1)}, u32[]{:S(2)}, u32[]{:S(2)}) collective-permute-start(f32[2,4,8,320]{3,2,1,0:T(8,128)S(1)} %get-tuple-element.240), channel_id=1, source_target_pairs={{0,4},{4,8},{8,12},{1,5},{5,9},{9,13},{2,6},{6,10},{10,14},{3,7},{... | collective-permute-start | bytes 245768 | tf_op jit(solution)/shard_map/ppermute | solution.py:14
  193.2 3.8 %collective-permute-done.34 = f32[2,16,4,320]{3,1,2,0:T(8,128)S(1)} collective-permute-done((f32[2,16,4,320]{3,1,2,0:T(8,128)S(1)}, f32[2,16,4,320]{3,1,2,0:T(8,128)S(1)}, u32[]{:S(2)}, u32[]{:S(2)}) %collective-permute-start.34) | collective-permute-done | bytes 163872 | tf_op jit(solution)/shard_map/ppermute | solution.py:14
  200.9 3.9 %collective-permute-start.36 = (f32[2,4,8,320]{3,2,1,0:T(8,128)S(1)}, f32[2,4,8,320]{3,2,1,0:T(8,128)S(1)}, u32[]{:S(2)}, u32[]{:S(2)}) collective-permute-start(f32[2,4,8,320]{3,2,1,0:T(8,128)S(1)} %get-tuple-element.238), channel_id=1, source_target_pairs={{0,4},{4,8},{8,12},{1,5},{5,9},{9,13},{2,6},{6,10},{10,14},{3,7},{... | collective-permute-start | bytes 245768 | tf_op jit(solution)/shard_map/ppermute | solution.py:14
  229.7 3.6 %collective-permute-done.38 = f32[2,16,4,320]{3,1,2,0:T(8,128)S(1)} collective-permute-done((f32[2,16,4,320]{3,1,2,0:T(8,128)S(1)}, f32[2,16,4,320]{3,1,2,0:T(8,128)S(1)}, u32[]{:S(2)}, u32[]{:S(2)}) %collective-permute-start.38) | collective-permute-done | bytes 163872 | tf_op jit(solution)/shard_map/ppermute | solution.py:14
  236.7 7.0 %fusion.361 = (f32[8,8,320]{2,1,0:T(8,128)}, f32[8,8,320]{2,1,0:T(8,128)}) fusion(f32[8,8,320]{2,1,0:T(8,128)S(1)} %multiply_add_fusion.1, f32[8,8,320]{2,1,0:T(8,128)S(1)} %multiply_add_fusion.3, f32[8,8,320]{2,1,0:T(8,128)S(1)} %multiply_add_fusion.4, f32[8,8,320]{2,1,0:T(8,128)S(1)} %multiply_add_fusion.8, f32[8,8,320]{2,1,0:T(8,128)S(1)} %copy-done.7, ...), kind=kLoop, calls=%fused_computation.864 | loop fusion | flops 1228800 | bytes 1556530 | tf_op jit(solution)/shard_map/add | solution.py:119
  (247 shorter events, 118.7 us)
Async XLA Ops:
  1.5 23.6 %collective-permute-start.1 = (f32[2,4,8,320]{3,2,1,0:T(8,128)S(1)}, f32[2,4,8,320]{3,2,1,0:T(8,128)S(1)}, u32[]{:S(2)}, u32[]{:S(2)}) collective-permute-start(f32[2,4,8,320]{3,2,1,0:T(8,128)S(1)} %get-tuple-element.257), channel_id=1, source_target_pairs={{4,0},{8,4},{12,8},{5,1},{9,5},{13,9},{6,2},{10,6},{14,10},{7,3},{... | collective-permute-start | bytes 245768 | tf_op jit(solution)/shard_map/ppermute | solution.py:17
  3.9 21.3 %collective-permute-start = (f32[2,4,8,320]{3,2,1,0:T(8,128)S(1)}, f32[2,4,8,320]{3,2,1,0:T(8,128)S(1)}, u32[]{:S(2)}, u32[]{:S(2)}) collective-permute-start(f32[2,4,8,320]{3,2,1,0:T(8,128)S(1)} %get-tuple-element.256), channel_id=1, source_target_pairs={{0,4},{4,8},{8,12},{1,5},{5,9},{9,13},{2,6},{6,10},{10,14},{3,7},{... | collective-permute-start | bytes 245768 | tf_op jit(solution)/shard_map/ppermute | solution.py:14
  8.2 22.2 %all-to-all-start = ((f32[16,1,640]{2,1,0:T(1,128)}), f32[16,1,640]{2,1,0:T(1,128)S(1)}, u32[]{:S(2)}, u32[]{:S(2)}) async-start(f32[16,1,640]{2,1,0:T(1,128)} %reshape.617), calls=%async_computation | async-start | bytes 81920 | tf_op jit(solution)/shard_map/all_to_all | solution.py:69
  25.3 12.8 %collective-permute-start.3 = (f32[2,16,4,320]{3,1,2,0:T(8,128)S(1)}, f32[2,16,4,320]{3,1,2,0:T(8,128)S(1)}, u32[]{:S(2)}, u32[]{:S(2)}) collective-permute-start(f32[2,16,4,320]{3,1,2,0:T(8,128)S(1)} %copy.930), channel_id=1, source_target_pairs={{1,0},{2,1},{3,2},{5,4},{6,5},{7,6},{9,8},{10,9},{11,10},{13,12},{... | collective-permute-start | bytes 491528 | tf_op jit(solution)/shard_map/ppermute | solution.py:17
  27.3 11.0 %collective-permute-start.2 = (f32[2,16,4,320]{3,1,2,0:T(8,128)S(1)}, f32[2,16,4,320]{3,1,2,0:T(8,128)S(1)}, u32[]{:S(2)}, u32[]{:S(2)}) collective-permute-start(f32[2,16,4,320]{3,1,2,0:T(8,128)S(1)} %copy.929), channel_id=1, source_target_pairs={{0,1},{1,2},{2,3},{4,5},{5,6},{6,7},{8,9},{9,10},{10,11},{12,13},{... | collective-permute-start | bytes 491528 | tf_op jit(solution)/shard_map/ppermute | solution.py:14
  41.5 6.5 %collective-permute-start.5 = (f32[2,4,8,320]{3,2,1,0:T(8,128)S(1)}, f32[2,4,8,320]{3,2,1,0:T(8,128)S(1)}, u32[]{:S(2)}, u32[]{:S(2)}) collective-permute-start(f32[2,4,8,320]{3,2,1,0:T(8,128)S(1)} %get-tuple-element.255), channel_id=1, source_target_pairs={{4,0},{8,4},{12,8},{5,1},{9,5},{13,9},{6,2},{10,6},{14,10},{7,3},{... | collective-permute-start | bytes 245768 | tf_op jit(solution)/shard_map/ppermute | solution.py:17
  44.9 6.5 %collective-permute-start.4 = (f32[2,4,8,320]{3,2,1,0:T(8,128)S(1)}, f32[2,4,8,320]{3,2,1,0:T(8,128)S(1)}, u32[]{:S(2)}, u32[]{:S(2)}) collective-permute-start(f32[2,4,8,320]{3,2,1,0:T(8,128)S(1)} %get-tuple-element.254), channel_id=1, source_target_pairs={{0,4},{4,8},{8,12},{1,5},{5,9},{9,13},{2,6},{6,10},{10,14},{3,7},{... | collective-permute-start | bytes 245768 | tf_op jit(solution)/shard_map/ppermute | solution.py:14
  53.8 7.0 %collective-permute-start.6 = (f32[2,16,4,320]{3,1,2,0:T(8,128)S(1)}, f32[2,16,4,320]{3,1,2,0:T(8,128)S(1)}, u32[]{:S(2)}, u32[]{:S(2)}) collective-permute-start(f32[2,16,4,320]{3,1,2,0:T(8,128)S(1)} %copy.931), channel_id=1, source_target_pairs={{0,1},{1,2},{2,3},{4,5},{5,6},{6,7},{8,9},{9,10},{10,11},{12,13},{... | collective-permute-start | bytes 491528 | tf_op jit(solution)/shard_map/ppermute | solution.py:14
  62.5 6.5 %collective-permute-start.9 = (f32[2,4,8,320]{3,2,1,0:T(8,128)S(1)}, f32[2,4,8,320]{3,2,1,0:T(8,128)S(1)}, u32[]{:S(2)}, u32[]{:S(2)}) collective-permute-start(f32[2,4,8,320]{3,2,1,0:T(8,128)S(1)} %get-tuple-element.253), channel_id=1, source_target_pairs={{4,0},{8,4},{12,8},{5,1},{9,5},{13,9},{6,2},{10,6},{14,10},{7,3},{... | collective-permute-start | bytes 245768 | tf_op jit(solution)/shard_map/ppermute | solution.py:17
  66.0 6.5 %collective-permute-start.8 = (f32[2,4,8,320]{3,2,1,0:T(8,128)S(1)}, f32[2,4,8,320]{3,2,1,0:T(8,128)S(1)}, u32[]{:S(2)}, u32[]{:S(2)}) collective-permute-start(f32[2,4,8,320]{3,2,1,0:T(8,128)S(1)} %get-tuple-element.252), channel_id=1, source_target_pairs={{0,4},{4,8},{8,12},{1,5},{5,9},{9,13},{2,6},{6,10},{10,14},{3,7},{... | collective-permute-start | bytes 245768 | tf_op jit(solution)/shard_map/ppermute | solution.py:14
  74.6 7.0 %collective-permute-start.10 = (f32[2,16,4,320]{3,1,2,0:T(8,128)S(1)}, f32[2,16,4,320]{3,1,2,0:T(8,128)S(1)}, u32[]{:S(2)}, u32[]{:S(2)}) collective-permute-start(f32[2,16,4,320]{3,1,2,0:T(8,128)S(1)} %copy.933), channel_id=1, source_target_pairs={{0,1},{1,2},{2,3},{4,5},{5,6},{6,7},{8,9},{9,10},{10,11},{12,13},{... | collective-permute-start | bytes 491528 | tf_op jit(solution)/shard_map/ppermute | solution.py:14
  83.3 6.5 %collective-permute-start.13 = (f32[2,4,8,320]{3,2,1,0:T(8,128)S(1)}, f32[2,4,8,320]{3,2,1,0:T(8,128)S(1)}, u32[]{:S(2)}, u32[]{:S(2)}) collective-permute-start(f32[2,4,8,320]{3,2,1,0:T(8,128)S(1)} %get-tuple-element.251), channel_id=1, source_target_pairs={{4,0},{8,4},{12,8},{5,1},{9,5},{13,9},{6,2},{10,6},{14,10},{7,3},{... | collective-permute-start | bytes 245768 | tf_op jit(solution)/shard_map/ppermute | solution.py:17
  85.2 6.5 %collective-permute-start.12 = (f32[2,4,8,320]{3,2,1,0:T(8,128)S(1)}, f32[2,4,8,320]{3,2,1,0:T(8,128)S(1)}, u32[]{:S(2)}, u32[]{:S(2)}) collective-permute-start(f32[2,4,8,320]{3,2,1,0:T(8,128)S(1)} %get-tuple-element.250), channel_id=1, source_target_pairs={{0,4},{4,8},{8,12},{1,5},{5,9},{9,13},{2,6},{6,10},{10,14},{3,7},{... | collective-permute-start | bytes 245768 | tf_op jit(solution)/shard_map/ppermute | solution.py:14
  93.8 7.0 %collective-permute-start.14 = (f32[2,16,4,320]{3,1,2,0:T(8,128)S(1)}, f32[2,16,4,320]{3,1,2,0:T(8,128)S(1)}, u32[]{:S(2)}, u32[]{:S(2)}) collective-permute-start(f32[2,16,4,320]{3,1,2,0:T(8,128)S(1)} %copy.935), channel_id=1, source_target_pairs={{0,1},{1,2},{2,3},{4,5},{5,6},{6,7},{8,9},{9,10},{10,11},{12,13},{... | collective-permute-start | bytes 491528 | tf_op jit(solution)/shard_map/ppermute | solution.py:14
  102.4 6.5 %collective-permute-start.17 = (f32[2,4,8,320]{3,2,1,0:T(8,128)S(1)}, f32[2,4,8,320]{3,2,1,0:T(8,128)S(1)}, u32[]{:S(2)}, u32[]{:S(2)}) collective-permute-start(f32[2,4,8,320]{3,2,1,0:T(8,128)S(1)} %get-tuple-element.249), channel_id=1, source_target_pairs={{4,0},{8,4},{12,8},{5,1},{9,5},{13,9},{6,2},{10,6},{14,10},{7,3},{... | collective-permute-start | bytes 245768 | tf_op jit(solution)/shard_map/ppermute | solution.py:17
  104.4 6.5 %collective-permute-start.16 = (f32[2,4,8,320]{3,2,1,0:T(8,128)S(1)}, f32[2,4,8,320]{3,2,1,0:T(8,128)S(1)}, u32[]{:S(2)}, u32[]{:S(2)}) collective-permute-start(f32[2,4,8,320]{3,2,1,0:T(8,128)S(1)} %get-tuple-element.248), channel_id=1, source_target_pairs={{0,4},{4,8},{8,12},{1,5},{5,9},{9,13},{2,6},{6,10},{10,14},{3,7},{... | collective-permute-start | bytes 245768 | tf_op jit(solution)/shard_map/ppermute | solution.py:14
  113.0 7.0 %collective-permute-start.18 = (f32[2,16,4,320]{3,1,2,0:T(8,128)S(1)}, f32[2,16,4,320]{3,1,2,0:T(8,128)S(1)}, u32[]{:S(2)}, u32[]{:S(2)}) collective-permute-start(f32[2,16,4,320]{3,1,2,0:T(8,128)S(1)} %copy.937), channel_id=1, source_target_pairs={{0,1},{1,2},{2,3},{4,5},{5,6},{6,7},{8,9},{9,10},{10,11},{12,13},{... | collective-permute-start | bytes 491528 | tf_op jit(solution)/shard_map/ppermute | solution.py:14
  132.2 7.0 %collective-permute-start.22 = (f32[2,16,4,320]{3,1,2,0:T(8,128)S(1)}, f32[2,16,4,320]{3,1,2,0:T(8,128)S(1)}, u32[]{:S(2)}, u32[]{:S(2)}) collective-permute-start(f32[2,16,4,320]{3,1,2,0:T(8,128)S(1)} %copy.939), channel_id=1, source_target_pairs={{0,1},{1,2},{2,3},{4,5},{5,6},{6,7},{8,9},{9,10},{10,11},{12,13},{... | collective-permute-start | bytes 491528 | tf_op jit(solution)/shard_map/ppermute | solution.py:14
  151.5 7.0 %collective-permute-start.26 = (f32[2,16,4,320]{3,1,2,0:T(8,128)S(1)}, f32[2,16,4,320]{3,1,2,0:T(8,128)S(1)}, u32[]{:S(2)}, u32[]{:S(2)}) collective-permute-start(f32[2,16,4,320]{3,1,2,0:T(8,128)S(1)} %copy.941), channel_id=1, source_target_pairs={{0,1},{1,2},{2,3},{4,5},{5,6},{6,7},{8,9},{9,10},{10,11},{12,13},{... | collective-permute-start | bytes 491528 | tf_op jit(solution)/shard_map/ppermute | solution.py:14
  170.8 7.0 %collective-permute-start.30 = (f32[2,16,4,320]{3,1,2,0:T(8,128)S(1)}, f32[2,16,4,320]{3,1,2,0:T(8,128)S(1)}, u32[]{:S(2)}, u32[]{:S(2)}) collective-permute-start(f32[2,16,4,320]{3,1,2,0:T(8,128)S(1)} %copy.943), channel_id=1, source_target_pairs={{0,1},{1,2},{2,3},{4,5},{5,6},{6,7},{8,9},{9,10},{10,11},{12,13},{... | collective-permute-start | bytes 491528 | tf_op jit(solution)/shard_map/ppermute | solution.py:14
  190.0 7.0 %collective-permute-start.34 = (f32[2,16,4,320]{3,1,2,0:T(8,128)S(1)}, f32[2,16,4,320]{3,1,2,0:T(8,128)S(1)}, u32[]{:S(2)}, u32[]{:S(2)}) collective-permute-start(f32[2,16,4,320]{3,1,2,0:T(8,128)S(1)} %copy.945), channel_id=1, source_target_pairs={{0,1},{1,2},{2,3},{4,5},{5,6},{6,7},{8,9},{9,10},{10,11},{12,13},{... | collective-permute-start | bytes 491528 | tf_op jit(solution)/shard_map/ppermute | solution.py:14
  198.8 25.5 %collective-permute-start.37 = (f32[2,4,8,320]{3,2,1,0:T(8,128)S(1)}, f32[2,4,8,320]{3,2,1,0:T(8,128)S(1)}, u32[]{:S(2)}, u32[]{:S(2)}) collective-permute-start(f32[2,4,8,320]{3,2,1,0:T(8,128)S(1)} %get-tuple-element.239), channel_id=1, source_target_pairs={{4,0},{8,4},{12,8},{5,1},{9,5},{13,9},{6,2},{10,6},{14,10},{7,3},{... | collective-permute-start | bytes 245768 | tf_op jit(solution)/shard_map/ppermute | solution.py:17
  200.9 23.5 %collective-permute-start.36 = (f32[2,4,8,320]{3,2,1,0:T(8,128)S(1)}, f32[2,4,8,320]{3,2,1,0:T(8,128)S(1)}, u32[]{:S(2)}, u32[]{:S(2)}) collective-permute-start(f32[2,4,8,320]{3,2,1,0:T(8,128)S(1)} %get-tuple-element.238), channel_id=1, source_target_pairs={{0,4},{4,8},{8,12},{1,5},{5,9},{9,13},{2,6},{6,10},{10,14},{3,7},{... | collective-permute-start | bytes 245768 | tf_op jit(solution)/shard_map/ppermute | solution.py:14
  226.4 7.0 %collective-permute-start.38 = (f32[2,16,4,320]{3,1,2,0:T(8,128)S(1)}, f32[2,16,4,320]{3,1,2,0:T(8,128)S(1)}, u32[]{:S(2)}, u32[]{:S(2)}) collective-permute-start(f32[2,16,4,320]{3,1,2,0:T(8,128)S(1)} %copy.947), channel_id=1, source_target_pairs={{0,1},{1,2},{2,3},{4,5},{5,6},{6,7},{8,9},{9,10},{10,11},{12,13},{... | collective-permute-start | bytes 491528 | tf_op jit(solution)/shard_map/ppermute | solution.py:14
  (31 other events, 241.0 us)
